TPU v7x, 256 devices: a whole 4x4x8 slice. The times are simulated.
256 devices in a mesh: dp: 8 (over x_lo, y), owner: 8 (over z), context: 4 (over x_hi, core).
Axes of the slice: x: 4 (x_hi: 2, x_lo: 2; x = x_hi * 2 + x_lo), y: 4, z: 8, core: 2. Of those that a mesh axis runs over, the one named last changes fastest.
Arguments:
- grad_partials: bfloat16 [32, 1536, 64, 192], P(('dp', 'context'), None, 'owner')
- assignment: int32 [64, 1], replicated, may hold values from 0 to 7; in each aligned block of 8 rows (0 to 7, 8 to 15, ...) at most 2 rows name the same one
- momentum: float32 [128, 1536, 192], P('owner', ('dp', 'context')), may hold values from -6 to 6
- q_weight: float32 [128, 1536, 192], P('owner', ('dp', 'context')), may hold values from -1.2 to 1.2
- k_weight: float32 [64, 512, 128], P('owner', ('dp', 'context')), may hold values from -6 to 6
- max_logits: float32 [4, 64], P('context'), may hold values from 20 to 400
Outputs:
- momentum_out: float32 [128, 1536, 192], P('owner', ('dp', 'context'))
- q_weight_out: float32 [128, 1536, 192], P('owner', ('dp', 'context'))
- k_weight_out: float32 [64, 512, 128], P('owner', ('dp', 'context'))
Inputs may be any that keep to these rules, and one draw needn't show every extreme that they name: `assignment`: in each aligned block of 8 heads no owner index is named more than 2 times, and some owner index exactly 2 times.
All inputs are finite; a program needn't handle non-finite values.
Results may differ from a plain program's by a relative error of at most 0.0007.
Values may be sent and summed in bfloat16 or wider, within the bound.
A program may use at most 128 MiB of HBM per device.

v0:
```python
import math
import jax
import jax.numpy as jnp
from jax import lax
from jax.sharding import PartitionSpec as P

QR = 1536
QK = 192
ITERS = 2
MOMENTUM_RATE = 0.95
WEIGHT_KEEP = 0.98
LOGIT_CAP = 100.0
QUINTIC_A = 3.4445
QUINTIC_B = -4.775
QUINTIC_C = 2.0315


def routing(assignment, heads_own, per_source):
    target = assignment[:, 0]
    head_index = jnp.arange(target.shape[0], dtype=jnp.int32)
    source_block = head_index // heads_own
    earlier = (
        (source_block[None, :] == source_block[:, None])
        & (head_index[None, :] < head_index[:, None])
        & (target[None, :] == target[:, None])
    )
    position = jnp.sum(earlier.astype(jnp.int32), axis=1)
    return (target, position, source_block * per_source + position)


def refresh(weight, orthogonal, gamma, kn_count):
    step_size = 0.04 * math.sqrt(max(QR, QK))
    column_index = jnp.arange(weight.shape[2])
    column_scale = jnp.where(
        column_index[None, :] < kn_count, jnp.sqrt(gamma)[:, None], gamma[:, None]
    )
    return (WEIGHT_KEEP * weight - step_size * orthogonal.astype(jnp.float32)) * column_scale[
        :, None, :
    ]


def quintic(whole):
    for step in range(ITERS):
        gram_matrix = jnp.einsum("nrk,nrl->nkl", whole, whole, preferred_element_type=jnp.float32)
        polynomial = (
            QUINTIC_B * gram_matrix
            + QUINTIC_C
            * jnp.einsum("nkl,nlm->nkm", gram_matrix, gram_matrix, precision=lax.Precision.HIGHEST)
        ).astype(jnp.bfloat16)
        whole = (
            QUINTIC_A * whole.astype(jnp.float32)
            + jnp.einsum("nrk,nkl->nrl", whole, polynomial, preferred_element_type=jnp.float32)
        ).astype(jnp.bfloat16)
    return whole


def orthogonalize(matrix):
    square_sum = lax.psum(jnp.sum(matrix * matrix, axis=(1, 2)), ("dp", "context"))
    iterate = (matrix / (jnp.sqrt(square_sum) + 1e-07)[:, None, None]).astype(jnp.bfloat16)
    row_count = matrix.shape[1]
    gathered = lax.all_gather(iterate, ("dp", "context"), axis=1, tiled=True)
    gathered = quintic(gathered)
    return lax.dynamic_slice_in_dim(
        gathered, lax.axis_index(("dp", "context")) * row_count, row_count, 1
    )


def body(grad_partials, assignment, momentum, q_weight, k_weight, max_logits):
    heads_own = grad_partials.shape[2]
    slots_own = momentum.shape[0]
    kn_count = k_weight.shape[2]
    per_source = slots_own // lax.axis_size("owner")
    my_owner = lax.axis_index("owner")
    target, position, local_slot = routing(assignment, heads_own, per_source)
    peak_logit = lax.pmax(max_logits[0], "context")
    gamma = jnp.minimum(1.0, LOGIT_CAP / peak_logit)
    partial_value = grad_partials[0]
    grad_rows = lax.psum_scatter(
        partial_value.astype(jnp.float32), ("dp", "context"), scatter_dimension=0, tiled=True
    )
    home_target = lax.dynamic_slice_in_dim(target, my_owner * heads_own, heads_own)
    home_position = lax.dynamic_slice_in_dim(position, my_owner * heads_own, heads_own)
    send_index = home_target * per_source + home_position
    slot_index = jnp.arange(slots_own, dtype=jnp.int32)
    sender = (slot_index[:, None] == send_index[None, :]).astype(jnp.float32)
    owned_mask = (
        (target[None, :] == my_owner) & (local_slot[None, :] == slot_index[:, None])
    ).astype(jnp.float32)
    occupied = (jnp.sum(owned_mask, axis=1) > 0.5)[:, None, None]
    home_gamma = lax.dynamic_slice_in_dim(gamma, my_owner * heads_own, heads_own)
    outgoing = jnp.einsum("qi,rik->qrk", sender, grad_rows, precision=lax.Precision.HIGHEST)
    arrived = lax.all_to_all(outgoing, "owner", split_axis=0, concat_axis=0, tiled=True)
    refreshed = jnp.where(occupied, MOMENTUM_RATE * momentum + arrived, momentum)
    orthogonal = orthogonalize(refreshed)
    slot_gamma = jnp.sum(owned_mask * gamma[None, :], axis=1)
    slot_gamma = jnp.where(occupied[:, 0, 0], slot_gamma, 1.0)
    q_weight_out = jnp.where(
        occupied, refresh(q_weight, orthogonal, slot_gamma, kn_count), q_weight
    )
    k_weight_out = k_weight * jnp.sqrt(home_gamma)[:, None, None]
    return (refreshed, q_weight_out, k_weight_out)


def solution(mesh):
    placed = (
        P(("dp", "context"), None, "owner", None),
        P(),
        P("owner", ("dp", "context"), None),
        P("owner", ("dp", "context"), None),
        P("owner", ("dp", "context"), None),
        P("context", None),
    )
    return jax.shard_map(
        body,
        mesh=mesh,
        in_specs=placed,
        out_specs=(
            P("owner", ("dp", "context"), None),
            P("owner", ("dp", "context"), None),
            P("owner", ("dp", "context"), None),
        ),
        check_vma=False,
    )
```

profile of v0, /device:TPU:1, one launch (start us, length us, event | category | flops | bytes accessed | tf_op | source)
XLA Modules:
  0.0 456.4 jit_solution(1013946448971146130)
XLA Ops:
  7.2 0.0 reduce-scatter.2.cloned.1.call-start
  7.2 9.2 %copy.57 = bf16[1,1536,8,192]{3,2,1,0:T(8,128)(2,1)} copy(bf16[1,1536,8,192]{1,3,2,0:T(8,128)(2,1)} %param.6) | data formatting | bytes 9437184 | tf_op args[0]
  16.4 7.5 %bitcast_convert_fusion = f32[1536,8,192]{2,1,0:T(8,128)} fusion(bf16[1,1536,8,192]{3,2,1,0:T(8,128)(2,1)} %copy.57), kind=kLoop, calls=%fused_computation.4 | loop fusion | flops 2359296 | bytes 14155776 | tf_op jit(solution)/shard_map/convert_element_type | solution.py:79
  23.8 0.0 copy-start.4
  23.8 0.0 reduce-scatter.2.cloned.1.call-update
  23.9 0.0 copy-start.5
  23.9 0.0 copy-start.1
  23.9 0.6 copy-done.4
  24.5 0.2 convert_reduce_fusion
  24.7 0.1 fusion.13
  24.7 175.2 %reduce-scatter.2.cloned.1.call-done = f32[48,8,192]{2,1,0:T(8,128)} async-done(((f32[1536,8,192]{2,1,0:T(8,128)}), f32[48,8,192]{2,1,0:T(8,128)}) %reduce-scatter.2.cloned.1.call-update) | async-done | bytes 294928 | tf_op jit(solution)/shard_map/reduce_scatter | solution.py:78
  199.9 1.6 fusion.8
  201.5 1.3 copy.58
  202.9 0.0 copy-start.3
  202.9 8.6 %all-to-all-start = ((f32[16,48,192]{2,1,0:T(8,128)}), f32[16,48,192]{2,1,0:T(8,128)S(1)}, u32[]{:S(2)}, u32[]{:S(2)}) async-start(f32[16,48,192]{2,1,0:T(8,128)} %copy.58), calls=%async_computation.1 | async-start | bytes 1572864 | tf_op jit(solution)/shard_map/all_to_all | solution.py:92
  211.5 0.0 all-gather.2.cloned.1.call-start
  211.5 0.0 copy-done.5
  211.5 10.9 %pmax.7 = f32[64]{0:T(128)S(1)} all-reduce(f32[64]{0:T(128)S(1)} %bitcast.24), channel_id=1, replica_groups=mesh['dp'=8,'owner'=8,'context'=4] {'context'}, use_global_device_ids=true, to_apply=%region_5.6 | all-reduce | flops 64 | bytes 512 | tf_op jit(solution)/shard_map/pmax | solution.py:75
  222.4 0.1 select_reduce_fusion
  222.5 8.9 %all-to-all-done = f32[16,48,192]{2,1,0:T(8,128)S(1)} async-done(((f32[16,48,192]{2,1,0:T(8,128)}), f32[16,48,192]{2,1,0:T(8,128)S(1)}, u32[]{:S(2)}, u32[]{:S(2)}) %all-to-all-start) | async-done | bytes 589856 | tf_op jit(solution)/shard_map/all_to_all | solution.py:92
  231.4 0.0 copy-done.1
  231.4 0.3 multiply_reduce_fusion
  231.7 0.0 copy-start
  231.8 66.2 %psum.7 = f32[16]{0:T(128)S(1)} all-reduce(f32[16]{0:T(128)S(1)} %get-tuple-element.16), channel_id=1, replica_groups=mesh['dp'=8,'owner'=8,'context'=4] {'dp','context'}, use_global_device_ids=true, to_apply=%region_4.5 | all-reduce | flops 16 | bytes 128 | tf_op jit(solution)/shard_map/psum | solution.py:58
  297.9 0.1 divide_convert_fusion
  298.1 0.9 copy.59
  298.9 0.0 all-gather.2.cloned.1.call-update
  299.0 0.1 dynamic-slice_sqrt_fusion
  299.1 0.1 broadcast_select_fusion
  299.1 0.0 copy-done.3
  299.1 0.7 broadcast_multiply_fusion
  299.9 73.1 %all-gather.2.cloned.1.call-done = bf16[16,1536,192]{2,0,1:T(8,128)(2,1)} async-done(((bf16[16,48,192]{2,0,1:T(8,128)(2,1)}), bf16[16,1536,192]{2,0,1:T(8,128)(2,1)}) %all-gather.2.cloned.1.call-update) | async-done | bytes 9437200 | tf_op jit(solution)/shard_map/all_gather | solution.py:61
  373.0 21.7 %fusion = f32[16,192,192]{2,1,0:T(8,128)S(1)} fusion(bf16[16,1536,192]{2,0,1:T(8,128)(2,1)} %all-gather.2.cloned.1.call-done), kind=kOutput, calls=%fused_computation.1 | convolution fusion | flops 1811939328 | bytes 11796480 | tf_op jit(solution)/shard_map/nrk,nrl->nkl/dot_general | solution.py:44
  394.7 0.0 copy-done
  394.7 3.6 add_convert_fusion.2
  398.3 17.7 %add_convert_fusion = bf16[16,1536,192]{2,1,0:T(8,128)(2,1)} fusion(bf16[16,192,192]{2,1,0:T(8,128)(2,1)S(1)} %add_convert_fusion.2, bf16[16,1536,192]{2,0,1:T(8,128)(2,1)} %all-gather.2.cloned.1.call-done), kind=kOutput, calls=%fused_computation | convolution fusion | flops 1830813696 | bytes 20054016 | tf_op jit(solution)/shard_map/nrk,nkl->nrl/dot_general | solution.py:52
  416.0 11.3 %fusion.15 = f32[16,192,192]{2,1,0:T(8,128)S(1)} fusion(bf16[16,1536,192]{2,1,0:T(8,128)(2,1)} %add_convert_fusion), kind=kOutput, calls=%fused_computation.44 | convolution fusion | flops 1811939328 | bytes 11796480 | tf_op jit(solution)/shard_map/nrk,nrl->nkl/dot_general | solution.py:44
  427.4 3.5 add_convert_fusion.1
  430.8 0.0 copy-start.2
  430.9 16.4 %fusion.16 = f32[16,1536,192]{2,1,0:T(8,128)} fusion(bf16[16,1536,192]{2,1,0:T(8,128)(2,1)} %add_convert_fusion, bf16[16,192,192]{2,1,0:T(8,128)(2,1)S(1)} %add_convert_fusion.1), kind=kOutput, calls=%fused_computation.45 | convolution fusion | flops 1811939328 | bytes 29491200 | tf_op jit(solution)/shard_map/nrk,nkl->nrl/dot_general | solution.py:52
  447.2 0.0 copy-done.2
  447.2 2.4 multiply_select_fusion
  (8 shorter events, 0.0 us)
Async XLA Ops:
  7.2 192.8 %reduce-scatter.2.cloned.1.call-start = ((), (), s32[]{:S(2)}) async-start(), calls=%async_computation.2 | async-start | bytes 12976128 | tf_op jit(solution)/shard_map/reduce_scatter | solution.py:78
  23.8 0.7 copy-start.4
  23.9 187.7 %copy-start.5 = (f32[1,64]{1,0:T(1,128)S(1)}, f32[1,64]{1,0:T(1,128)}, u32[]{:S(2)}) copy-start(f32[1,64]{1,0:T(1,128)} %param.11) | copy-start | bytes 772
  23.9 207.6 %copy-start.1 = (f32[16,48,192]{2,1,0:T(8,128)S(1)}, f32[16,48,192]{2,1,0:T(8,128)}, u32[]{:S(2)}) copy-start(f32[16,48,192]{2,1,0:T(8,128)} %param.8) | copy-start | bytes 1769476
  202.9 96.3 %copy-start.3 = (f32[8,16,128]{2,1,0:T(8,128)S(1)}, f32[8,16,128]{2,1,0:T(8,128)}, u32[]{:S(2)}) copy-start(f32[8,16,128]{2,1,0:T(8,128)} %param.10) | copy-start | bytes 196612
  202.9 28.6 %all-to-all-start = ((f32[16,48,192]{2,1,0:T(8,128)}), f32[16,48,192]{2,1,0:T(8,128)S(1)}, u32[]{:S(2)}, u32[]{:S(2)}) async-start(f32[16,48,192]{2,1,0:T(8,128)} %copy.58), calls=%async_computation.1 | async-start | bytes 1572864 | tf_op jit(solution)/shard_map/all_to_all | solution.py:92
  211.5 161.5 %all-gather.2.cloned.1.call-start = ((), (), s32[]{:S(2)}) async-start(), calls=%async_computation.3 | async-start | bytes 12976128 | tf_op jit(solution)/shard_map/all_gather | solution.py:61
  231.7 163.0 %copy-start = (f32[16,48,192]{2,1,0:T(8,128)}, f32[16,48,192]{2,1,0:T(8,128)S(1)}, u32[]{:S(2)}) copy-start(f32[16,48,192]{2,1,0:T(8,128)S(1)} %get-tuple-element.17) | copy-start | bytes 1769476
  430.8 16.4 %copy-start.2 = (f32[16,48,192]{2,1,0:T(8,128)S(1)}, f32[16,48,192]{2,1,0:T(8,128)}, u32[]{:S(2)}) copy-start(f32[16,48,192]{2,1,0:T(8,128)} %param.9) | copy-start | bytes 1769476
Sparse Core Ops, SparseCore 0:
  24.0 175.8 reduce-scatter.1
  299.1 73.8 all-gather.1
where the time goes:
time: 457 us; the launch traced here: 456 us
  waiting for transfers between devices  257 us (56%)
  blocking collectives  77 us (17%)
  matrix products  75.8 us (17%)
  between operations  14.2 us (3%)
  local copies, waits for them, and re-layouts  12.1 us (3%)
  other arithmetic  11.5 us (3%)
  starting transfers between devices  8.69 us (2%)
    reduce_scatter x1, waiting for transfers between devices, body(): lax.psum_scatter(partial_value.astype(jnp.float32), ('dp', 'context'), sc...  175 us
    all_gather x1, waiting for transfers between devices, orthogonalize(): gathered = lax.all_gather(iterate, ('dp', 'context'), axis=1, tiled=True)  73.1 us
    psum x1, blocking collectives, orthogonalize(): lax.psum(jnp.sum(matrix * matrix, axis=(1, 2)), ('dp', 'context'))  66.2 us
    dot_general x2, matrix products, quintic(): jnp.einsum('nrk,nkl->nrl', whole, polynomial, preferred_element_type=jnp....  34.1 us
    dot_general x2, matrix products, quintic(): jnp.einsum('nrk,nrl->nkl', whole, whole, preferred_element_type=jnp.float32)  33.1 us
    pmax x1, blocking collectives, body(): peak_logit = lax.pmax(max_logits[0], 'context')  10.9 us
    unnamed x13, local copies, waits for them, and re-layouts  9.79 us
  transfers between devices with their start and end apart: 3, of which 3 were waited for; matrix products, arithmetic and copies ran while one was open for 0% of the time, Pallas kernels for 0%

commit v1 on v0

--- a/solution.py
+++ b/solution.py
@@ -13,6 +13,11 @@
 QUINTIC_A = 3.4445
 QUINTIC_B = -4.775
 QUINTIC_C = 2.0315
+
+
+def axis_by_axis(x, inner_axis, outer_axis):
+    partial = lax.psum(x, inner_axis)
+    return lax.psum(partial, outer_axis)
 
 
 def routing(assignment, heads_own, per_source):
@@ -55,7 +60,7 @@
 
 
 def orthogonalize(matrix):
-    square_sum = lax.psum(jnp.sum(matrix * matrix, axis=(1, 2)), ("dp", "context"))
+    square_sum = axis_by_axis(jnp.sum(matrix * matrix, axis=(1, 2)), "context", "dp")
     iterate = (matrix / (jnp.sqrt(square_sum) + 1e-07)[:, None, None]).astype(jnp.bfloat16)
     row_count = matrix.shape[1]
     gathered = lax.all_gather(iterate, ("dp", "context"), axis=1, tiled=True)

time: 457 us -> 419 us (0.917)
  blocking collectives: 77 us -> 35.1 us
    psum x1 -> x2, blocking collectives: 66.2 us -> 24.2 us  [the longest x1 13.5 us: axis_by_axis(): return lax.psum(partial, outer_axis)]
where the time goes in v1:
time: 419 us; the launch traced here: 418 us
  waiting for transfers between devices  261 us (62%)
  matrix products  75.8 us (18%)
  blocking collectives  35.1 us (8%)
  between operations  14.2 us (3%)
  local copies, waits for them, and re-layouts  12.1 us (3%)
  other arithmetic  11.5 us (3%)
  starting transfers between devices  8.69 us (2%)
    reduce_scatter x1, waiting for transfers between devices, body(): lax.psum_scatter(partial_value.astype(jnp.float32), ('dp', 'context'), sc...  175 us
    all_gather x1, waiting for transfers between devices, orthogonalize(): gathered = lax.all_gather(iterate, ('dp', 'context'), axis=1, tiled=True)  76.8 us
    dot_general x2, matrix products, quintic(): jnp.einsum('nrk,nkl->nrl', whole, polynomial, preferred_element_type=jnp....  34.1 us
    dot_general x2, matrix products, quintic(): jnp.einsum('nrk,nrl->nkl', whole, whole, preferred_element_type=jnp.float32)  33.1 us
    psum x1, blocking collectives, axis_by_axis(): return lax.psum(partial, outer_axis)  13.5 us
    pmax x1, blocking collectives, body(): peak_logit = lax.pmax(max_logits[0], 'context')  10.9 us
    psum x1, blocking collectives, axis_by_axis(): partial = lax.psum(x, inner_axis)  10.7 us
    unnamed x13, local copies, waits for them, and re-layouts  9.79 us
  transfers between devices with their start and end apart: 3, of which 3 were waited for; matrix products, arithmetic and copies ran while one was open for 0% of the time, Pallas kernels for 0%

profile of v1, /device:TPU:1, one launch (start us, length us, event | category | flops | bytes accessed | tf_op | source)
XLA Modules:
  0.0 418.2 jit_solution(2990450678348707835)
XLA Ops:
  7.2 0.0 reduce-scatter.2.cloned.1.call-start
  7.2 9.2 %copy.57 = bf16[1,1536,8,192]{3,2,1,0:T(8,128)(2,1)} copy(bf16[1,1536,8,192]{1,3,2,0:T(8,128)(2,1)} %param.6) | data formatting | bytes 9437184 | tf_op args[0]
  16.4 7.5 %bitcast_convert_fusion = f32[1536,8,192]{2,1,0:T(8,128)} fusion(bf16[1,1536,8,192]{3,2,1,0:T(8,128)(2,1)} %copy.57), kind=kLoop, calls=%fused_computation.4 | loop fusion | flops 2359296 | bytes 14155776 | tf_op jit(solution)/shard_map/convert_element_type | solution.py:84
  23.8 0.0 copy-start.4
  23.8 0.0 reduce-scatter.2.cloned.1.call-update
  23.9 0.0 copy-start.5
  23.9 0.0 copy-start.1
  23.9 0.6 copy-done.4
  24.5 0.2 convert_reduce_fusion
  24.7 0.1 fusion.13
  24.7 175.2 %reduce-scatter.2.cloned.1.call-done = f32[48,8,192]{2,1,0:T(8,128)} async-done(((f32[1536,8,192]{2,1,0:T(8,128)}), f32[48,8,192]{2,1,0:T(8,128)}) %reduce-scatter.2.cloned.1.call-update) | async-done | bytes 294928 | tf_op jit(solution)/shard_map/reduce_scatter | solution.py:83
  199.9 1.6 fusion.8
  201.5 1.3 copy.58
  202.9 0.0 copy-start.3
  202.9 8.6 %all-to-all-start = ((f32[16,48,192]{2,1,0:T(8,128)}), f32[16,48,192]{2,1,0:T(8,128)S(1)}, u32[]{:S(2)}, u32[]{:S(2)}) async-start(f32[16,48,192]{2,1,0:T(8,128)} %copy.58), calls=%async_computation.1 | async-start | bytes 1572864 | tf_op jit(solution)/shard_map/all_to_all | solution.py:97
  211.5 0.0 all-gather.2.cloned.1.call-start
  211.5 0.0 copy-done.5
  211.5 10.9 %pmax.7 = f32[64]{0:T(128)S(1)} all-reduce(f32[64]{0:T(128)S(1)} %bitcast.24), channel_id=1, replica_groups=mesh['dp'=8,'owner'=8,'context'=4] {'context'}, use_global_device_ids=true, to_apply=%region_6.7 | all-reduce | flops 64 | bytes 512 | tf_op jit(solution)/shard_map/pmax | solution.py:80
  222.4 0.1 select_reduce_fusion
  222.5 8.9 %all-to-all-done = f32[16,48,192]{2,1,0:T(8,128)S(1)} async-done(((f32[16,48,192]{2,1,0:T(8,128)}), f32[16,48,192]{2,1,0:T(8,128)S(1)}, u32[]{:S(2)}, u32[]{:S(2)}) %all-to-all-start) | async-done | bytes 589856 | tf_op jit(solution)/shard_map/all_to_all | solution.py:97
  231.4 0.0 copy-done.1
  231.4 0.3 multiply_reduce_fusion
  231.7 0.0 copy-start
  231.8 10.7 %psum.14 = f32[16]{0:T(128)S(1)} all-reduce(f32[16]{0:T(128)S(1)} %get-tuple-element.16), channel_id=1, replica_groups=mesh['dp'=8,'owner'=8,'context'=4] {'context'}, use_global_device_ids=true, to_apply=%region_4.5 | all-reduce | flops 16 | bytes 128 | tf_op jit(solution)/shard_map/psum | solution.py:19
  242.4 13.5 %psum.15 = f32[16]{0:T(128)S(1)} all-reduce(f32[16]{0:T(128)S(1)} %psum.14), channel_id=1, replica_groups=mesh['dp'=8,'owner'=8,'context'=4] {'dp'}, use_global_device_ids=true, to_apply=%region_5.6 | all-reduce | flops 16 | bytes 128 | tf_op jit(solution)/shard_map/psum | solution.py:20
  256.0 0.1 divide_convert_fusion
  256.1 0.9 copy.59
  257.0 0.0 all-gather.2.cloned.1.call-update
  257.0 0.1 dynamic-slice_sqrt_fusion
  257.1 0.1 broadcast_select_fusion
  257.2 0.0 copy-done.3
  257.2 0.7 broadcast_multiply_fusion
  257.9 76.8 %all-gather.2.cloned.1.call-done = bf16[16,1536,192]{2,0,1:T(8,128)(2,1)} async-done(((bf16[16,48,192]{2,0,1:T(8,128)(2,1)}), bf16[16,1536,192]{2,0,1:T(8,128)(2,1)}) %all-gather.2.cloned.1.call-update) | async-done | bytes 9437200 | tf_op jit(solution)/shard_map/all_gather | solution.py:66
  334.7 21.7 %fusion = f32[16,192,192]{2,1,0:T(8,128)S(1)} fusion(bf16[16,1536,192]{2,0,1:T(8,128)(2,1)} %all-gather.2.cloned.1.call-done), kind=kOutput, calls=%fused_computation.1 | convolution fusion | flops 1811939328 | bytes 11796480 | tf_op jit(solution)/shard_map/nrk,nrl->nkl/dot_general | solution.py:49
  356.4 0.0 copy-done
  356.4 3.6 add_convert_fusion.2
  360.1 17.7 %add_convert_fusion = bf16[16,1536,192]{2,1,0:T(8,128)(2,1)} fusion(bf16[16,192,192]{2,1,0:T(8,128)(2,1)S(1)} %add_convert_fusion.2, bf16[16,1536,192]{2,0,1:T(8,128)(2,1)} %all-gather.2.cloned.1.call-done), kind=kOutput, calls=%fused_computation | convolution fusion | flops 1830813696 | bytes 20054016 | tf_op jit(solution)/shard_map/nrk,nkl->nrl/dot_general | solution.py:57
  377.8 11.3 %fusion.15 = f32[16,192,192]{2,1,0:T(8,128)S(1)} fusion(bf16[16,1536,192]{2,1,0:T(8,128)(2,1)} %add_convert_fusion), kind=kOutput, calls=%fused_computation.44 | convolution fusion | flops 1811939328 | bytes 11796480 | tf_op jit(solution)/shard_map/nrk,nrl->nkl/dot_general | solution.py:49
  389.1 3.5 add_convert_fusion.1
  392.6 0.0 copy-start.2
  392.6 16.4 %fusion.16 = f32[16,1536,192]{2,1,0:T(8,128)} fusion(bf16[16,1536,192]{2,1,0:T(8,128)(2,1)} %add_convert_fusion, bf16[16,192,192]{2,1,0:T(8,128)(2,1)S(1)} %add_convert_fusion.1), kind=kOutput, calls=%fused_computation.45 | convolution fusion | flops 1811939328 | bytes 29491200 | tf_op jit(solution)/shard_map/nrk,nkl->nrl/dot_general | solution.py:57
  408.9 0.0 copy-done.2
  409.0 2.4 multiply_select_fusion
  (8 shorter events, 0.0 us)
Async XLA Ops:
  7.2 192.8 %reduce-scatter.2.cloned.1.call-start = ((), (), s32[]{:S(2)}) async-start(), calls=%async_computation.2 | async-start | bytes 12976128 | tf_op jit(solution)/shard_map/reduce_scatter | solution.py:83
  23.8 0.7 copy-start.4
  23.9 187.7 %copy-start.5 = (f32[1,64]{1,0:T(1,128)S(1)}, f32[1,64]{1,0:T(1,128)}, u32[]{:S(2)}) copy-start(f32[1,64]{1,0:T(1,128)} %param.11) | copy-start | bytes 772
  23.9 207.6 %copy-start.1 = (f32[16,48,192]{2,1,0:T(8,128)S(1)}, f32[16,48,192]{2,1,0:T(8,128)}, u32[]{:S(2)}) copy-start(f32[16,48,192]{2,1,0:T(8,128)} %param.8) | copy-start | bytes 1769476
  202.9 54.3 %copy-start.3 = (f32[8,16,128]{2,1,0:T(8,128)S(1)}, f32[8,16,128]{2,1,0:T(8,128)}, u32[]{:S(2)}) copy-start(f32[8,16,128]{2,1,0:T(8,128)} %param.10) | copy-start | bytes 196612
  202.9 28.6 %all-to-all-start = ((f32[16,48,192]{2,1,0:T(8,128)}), f32[16,48,192]{2,1,0:T(8,128)S(1)}, u32[]{:S(2)}, u32[]{:S(2)}) async-start(f32[16,48,192]{2,1,0:T(8,128)} %copy.58), calls=%async_computation.1 | async-start | bytes 1572864 | tf_op jit(solution)/shard_map/all_to_all | solution.py:97
  211.5 123.2 %all-gather.2.cloned.1.call-start = ((), (), s32[]{:S(2)}) async-start(), calls=%async_computation.3 | async-start | bytes 12976128 | tf_op jit(solution)/shard_map/all_gather | solution.py:66
  231.7 124.7 %copy-start = (f32[16,48,192]{2,1,0:T(8,128)}, f32[16,48,192]{2,1,0:T(8,128)S(1)}, u32[]{:S(2)}) copy-start(f32[16,48,192]{2,1,0:T(8,128)S(1)} %get-tuple-element.17) | copy-start | bytes 1769476
  392.6 16.4 %copy-start.2 = (f32[16,48,192]{2,1,0:T(8,128)S(1)}, f32[16,48,192]{2,1,0:T(8,128)}, u32[]{:S(2)}) copy-start(f32[16,48,192]{2,1,0:T(8,128)} %param.9) | copy-start | bytes 1769476
Sparse Core Ops, SparseCore 0:
  24.0 175.8 reduce-scatter.1
  257.1 77.5 all-gather.1
